TPU v7x, 256 devices: a whole 4x4x8 slice. The times are simulated.
256 devices in a mesh: seq: 32 (over z, y), head: 8 (over x, core).
Axes of the slice: x: 4, y: 4, z: 8, core: 2. Of those that a mesh axis runs over, the one named last changes fastest.
Arguments:
- queries: bfloat16 [32768, 8192], P(('seq', 'head')), may hold values from -18 to 18
- keys: bfloat16 [32768, 1024], P(('seq', 'head')), may hold values from -6 to 6
- values: bfloat16 [32768, 1024], P(('seq', 'head')), may hold values from -6 to 6
- upstream: bfloat16 [32768, 8192], P(('seq', 'head')), may hold values from -96 to 96
- send_rows: int32 [32, 1536], P('seq'), may hold values from -1 to 1023, as said below
- recv_rows: int32 [32, 1024], P('seq'), may hold values from 0 to 1535, as said below
- doc_lengths: int32 [32, 4], P('seq'), may hold values from 1 to 512, 1024 in all within a row
- pair_docs: int32 [128], replicated, may hold values from 0 to 127, each once
- response_mask: int32 [32768], P('seq'), may hold values 0 or 1
- policy_logp: float32 [32768], P('seq'), may hold values from -2.5 to -0.05
- ref_logp: float32 [32768], P('seq'), may hold values from -2.5 to -0.05
Outputs:
- grad_queries: bfloat16 [32768, 8192], P(('seq', 'head'))
- key_row_gradient: bfloat16 [32768, 1024], P(('seq', 'head'))
- value_row_gradient: bfloat16 [32768, 1024], P(('seq', 'head'))
Inputs may be any that keep to these rules, and one draw needn't show every extreme that they name: `send_rows`: entry o * 48 + k of loader group s names the row (of its 1024) that owner group o takes as its k-th row from s, or -1 for an empty slot. Every row of a loader group is named exactly once; in each block of 48 entries the named rows come first; every loader group fills some block completely. `recv_rows`: entry p of owner group o names the received slot s * 48 + k (k-th slot from loader group s) that holds its row p. The named slots of an owner group are distinct and are exactly the filled ones. `doc_lengths`: row o lists the lengths of owner group o's 4 dialogues in the order in which they fill its 1024 rows; each row sums to 1024. Dialogue j of owner group o has the number o * 4 + j. Pair k is the chosen dialogue pair_docs[2k] and the rejected dialogue pair_docs[2k+1]. `response_mask`: 1 marks a response token.
All inputs are finite; a program needn't handle non-finite values. No bound on the sum of `response_mask` on one device may be relied on, other than what follows from the above.
Results may differ from a plain program's by a relative error of at most 0.0088.
Values may be sent and summed in bfloat16 or wider, within the bound.
No kernel may reach another device: no remote copies, remote signals or barrier semaphores. Data moves between devices by JAX's collectives and lax.ppermute only.
A program may use at most 128 MiB of HBM per device.

v0:
```python
import math

import jax
import jax.numpy as jnp
from jax import lax
from jax.sharding import PartitionSpec as P

HEAD_SIZE = 128


dpo_beta = 0.1


def head_grads(query_block, key_block, value_block, grad_block, allowed, score_scale):
    scores = (
        lax.dot_general(
            query_block, key_block, (((1,), (1,)), ((), ())), preferred_element_type=jnp.float32
        )
        * score_scale
    )
    scores = jnp.where(allowed, scores, -1e30)
    highest = jnp.max(scores, axis=1, keepdims=True)
    lifted = jnp.exp(scores - highest)
    probs = lifted / jnp.sum(lifted, axis=1, keepdims=True)
    probs_low = probs.astype(jnp.bfloat16)
    output = jnp.dot(probs_low, value_block, preferred_element_type=jnp.float32)
    row_dot = jnp.sum(grad_block.astype(jnp.float32) * output, axis=1, keepdims=True)
    value_gradient = lax.dot_general(
        probs_low, grad_block, (((0,), (0,)), ((), ())), preferred_element_type=jnp.float32
    )
    grad_probs = lax.dot_general(
        grad_block, value_block, (((1,), (1,)), ((), ())), preferred_element_type=jnp.float32
    )
    grad_scores = (probs * (grad_probs - row_dot) * score_scale).astype(jnp.bfloat16)
    grad_query = jnp.dot(grad_scores, key_block, preferred_element_type=jnp.float32).astype(
        jnp.bfloat16
    )
    key_gradient = lax.dot_general(
        grad_scores, query_block, (((0,), (0,)), ((), ())), preferred_element_type=jnp.float32
    )
    return (grad_query, key_gradient, value_gradient)


def body(
    queries,
    keys,
    values,
    upstream,
    send_rows,
    recv_rows,
    doc_lengths,
    pair_docs,
    response_mask,
    policy_logp,
    ref_logp,
):
    tok_rows = queries.shape[0]
    head_devices = lax.axis_size("head")
    group_rows = tok_rows * head_devices
    query_width = queries.shape[1]
    shared_heads = keys.shape[1] // HEAD_SIZE
    copies = query_width // keys.shape[1]
    key_send = jnp.broadcast_to(
        keys.reshape(tok_rows, shared_heads, 1, HEAD_SIZE),
        (tok_rows, shared_heads, copies, HEAD_SIZE),
    ).reshape(tok_rows, query_width)
    value_send = jnp.broadcast_to(
        values.reshape(tok_rows, shared_heads, 1, HEAD_SIZE),
        (tok_rows, shared_heads, copies, HEAD_SIZE),
    ).reshape(tok_rows, query_width)
    query_group, upstream_group, key_group, value_group = (
        lax.all_to_all(queries, "head", split_axis=1, concat_axis=0, tiled=True),
        lax.all_to_all(upstream, "head", split_axis=1, concat_axis=0, tiled=True),
        lax.all_to_all(key_send, "head", split_axis=1, concat_axis=0, tiled=True),
        lax.all_to_all(value_send, "head", split_axis=1, concat_axis=0, tiled=True),
    )
    slot_rows = send_rows[0]
    filled = slot_rows >= 0
    safe_rows = jnp.where(filled, slot_rows, 0)

    def pack_rows(block):
        return jnp.where(
            filled[:, None], jnp.take(block, safe_rows, axis=0), jnp.zeros((), block.dtype)
        )

    arrived = (
        lax.all_to_all(pack_rows(query_group), "seq", split_axis=0, concat_axis=0, tiled=True),
        lax.all_to_all(pack_rows(upstream_group), "seq", split_axis=0, concat_axis=0, tiled=True),
        lax.all_to_all(pack_rows(key_group), "seq", split_axis=0, concat_axis=0, tiled=True),
        lax.all_to_all(pack_rows(value_group), "seq", split_axis=0, concat_axis=0, tiled=True),
    )
    where_from = recv_rows[0]
    query_own = jnp.take(arrived[0], where_from, axis=0)
    upstream_own = jnp.take(arrived[1], where_from, axis=0)
    key_own = jnp.take(arrived[2], where_from, axis=0)
    value_own = jnp.take(arrived[3], where_from, axis=0)
    owner_index = lax.axis_index("seq")
    doc_len = doc_lengths[0]
    doc_count = doc_len.shape[0]
    doc_ends = jnp.cumsum(doc_len)
    position = jnp.arange(group_rows, dtype=jnp.int32)
    doc_of_row = jnp.sum((position[:, None] >= doc_ends[None, :]).astype(jnp.int32), axis=1)
    member = doc_of_row[:, None] == jnp.arange(doc_count, dtype=jnp.int32)[None, :]
    token_gap = response_mask.astype(jnp.float32) * (policy_logp - ref_logp)
    doc_gap = jnp.sum(jnp.where(member, token_gap[:, None], 0.0), axis=0)
    global_doc = owner_index * doc_count + jnp.arange(doc_count, dtype=jnp.int32)
    total_docs = pair_docs.shape[0]
    pair_count = total_docs // 2
    slot_of = jnp.sum(
        jnp.where(
            pair_docs[None, :] == global_doc[:, None],
            jnp.arange(total_docs, dtype=jnp.int32)[None, :],
            0,
        ),
        axis=1,
    )
    pair_of = slot_of // 2
    doc_sign = 1.0 - 2.0 * (slot_of % 2).astype(jnp.float32)
    in_pair = pair_of[:, None] == jnp.arange(pair_count, dtype=jnp.int32)[None, :]
    pair_terms = jnp.sum(jnp.where(in_pair, (doc_sign * doc_gap)[:, None], 0.0), axis=0)
    owned_sum = lax.psum_scatter(pair_terms, "seq", scatter_dimension=0, tiled=True)
    owned_weight = dpo_beta * jax.nn.sigmoid(-dpo_beta * owned_sum)
    pair_weight = lax.all_gather(owned_weight, "seq", axis=0, tiled=True)
    doc_weight = jnp.sum(jnp.where(in_pair, pair_weight[None, :], 0.0), axis=1)
    doc_coef = -doc_sign * doc_weight
    row_coef = jnp.sum(jnp.where(member, doc_coef[None, :], 0.0), axis=1)
    grad_out = (row_coef[:, None] * upstream_own.astype(jnp.float32)).astype(jnp.bfloat16)
    allowed = (doc_of_row[:, None] == doc_of_row[None, :]) & (
        position[None, :] <= position[:, None]
    )
    heads_here = query_own.shape[1] // HEAD_SIZE
    kv_here = key_own.shape[1] // HEAD_SIZE
    per_shared = heads_here // kv_here
    score_scale = 1.0 / math.sqrt(HEAD_SIZE)

    def one_head(head_index, carry):
        grad_query, key_gradient, value_gradient = carry
        shared = head_index // per_shared
        query_block = lax.dynamic_slice_in_dim(query_own, head_index * HEAD_SIZE, HEAD_SIZE, 1)
        grad_block = lax.dynamic_slice_in_dim(grad_out, head_index * HEAD_SIZE, HEAD_SIZE, 1)
        key_block = lax.dynamic_slice_in_dim(key_own, shared * HEAD_SIZE, HEAD_SIZE, 1)
        value_block = lax.dynamic_slice_in_dim(value_own, shared * HEAD_SIZE, HEAD_SIZE, 1)
        head_query, head_key, head_value = head_grads(
            query_block, key_block, value_block, grad_block, allowed, score_scale
        )
        grad_query = lax.dynamic_update_slice_in_dim(
            grad_query, head_query, head_index * HEAD_SIZE, 1
        )
        key_gradient = lax.dynamic_update_slice_in_dim(
            key_gradient,
            lax.dynamic_slice_in_dim(key_gradient, shared * HEAD_SIZE, HEAD_SIZE, 1) + head_key,
            shared * HEAD_SIZE,
            1,
        )
        value_gradient = lax.dynamic_update_slice_in_dim(
            value_gradient,
            lax.dynamic_slice_in_dim(value_gradient, shared * HEAD_SIZE, HEAD_SIZE, 1) + head_value,
            shared * HEAD_SIZE,
            1,
        )
        return (grad_query, key_gradient, value_gradient)

    start_state = (
        jnp.zeros((group_rows, heads_here * HEAD_SIZE), jnp.bfloat16),
        jnp.zeros((group_rows, kv_here * HEAD_SIZE), jnp.float32),
        jnp.zeros((group_rows, kv_here * HEAD_SIZE), jnp.float32),
    )
    grad_query, key_gradient, value_gradient = lax.fori_loop(0, heads_here, one_head, start_state)
    local_shared = shared_heads // head_devices
    key_gradient = (
        key_gradient.reshape(group_rows, local_shared, kv_here // local_shared, HEAD_SIZE)
        .sum(axis=2)
        .reshape(group_rows, local_shared * HEAD_SIZE)
        .astype(jnp.bfloat16)
    )
    value_gradient = (
        value_gradient.reshape(group_rows, local_shared, kv_here // local_shared, HEAD_SIZE)
        .sum(axis=2)
        .reshape(group_rows, local_shared * HEAD_SIZE)
        .astype(jnp.bfloat16)
    )
    slot_count = slot_rows.shape[0]

    def spread_rows(block):
        return jnp.zeros((slot_count, block.shape[1]), block.dtype).at[where_from].set(block)

    returned = (
        lax.all_to_all(spread_rows(grad_query), "seq", split_axis=0, concat_axis=0, tiled=True),
        lax.all_to_all(spread_rows(key_gradient), "seq", split_axis=0, concat_axis=0, tiled=True),
        lax.all_to_all(spread_rows(value_gradient), "seq", split_axis=0, concat_axis=0, tiled=True),
    )
    target_rows = jnp.where(filled, slot_rows, group_rows)

    def place_rows(block):
        return (
            jnp.zeros((group_rows, block.shape[1]), block.dtype)
            .at[target_rows]
            .set(block, mode="drop")
        )

    final_query, final_key, final_value = (
        lax.all_to_all(place_rows(returned[0]), "head", split_axis=0, concat_axis=1, tiled=True),
        lax.all_to_all(place_rows(returned[1]), "head", split_axis=0, concat_axis=1, tiled=True),
        lax.all_to_all(place_rows(returned[2]), "head", split_axis=0, concat_axis=1, tiled=True),
    )
    return (final_query, final_key, final_value)


def solution(mesh):
    return jax.shard_map(
        body,
        mesh=mesh,
        in_specs=(
            P(("seq", "head"), None),
            P(("seq", "head"), None),
            P(("seq", "head"), None),
            P(("seq", "head"), None),
            P("seq", None),
            P("seq", None),
            P("seq", None),
            P(),
            P("seq"),
            P("seq"),
            P("seq"),
        ),
        out_specs=(P(("seq", "head"), None), P(("seq", "head"), None), P(("seq", "head"), None)),
        check_vma=False,
    )
```

profile of v0, /device:TPU:1, one launch (start us, length us, event | category | flops | bytes accessed | tf_op | source)
XLA Modules:
  0.0 967.0 jit_solution(1875019657296545672)
XLA Ops:
  4.3 6.7 all-to-all-start.2
  12.7 4.2 all_to_all.175
  16.8 20.4 %all-to-all-done.2 = bf16[128,8,1024]{2,0,1:T(8,128)(2,1)S(1)} async-done(((bf16[128,8,1024]{2,0,1:T(8,128)(2,1)}), bf16[128,8,1024]{2,0,1:T(8,128)(2,1)S(1)}, u32[]{:S(2)}, u32[]{:S(2)}) %all-to-all-start.2) | async-done | bytes 2097184 | tf_op jit(solution)/shard_map/all_to_all | solution.py:74
  37.2 5.2 all-to-all-start.6
  42.4 3.1 copy.85
  45.5 23.2 %all-to-all-done.6 = bf16[128,8,1024]{2,0,1:T(8,128)(2,1)} async-done(((bf16[128,8,1024]{2,0,1:T(8,128)(2,1)}), bf16[128,8,1024]{2,0,1:T(8,128)(2,1)}, u32[]{:S(2)}, u32[]{:S(2)}) %all-to-all-start.6) | async-done | bytes 2097184 | tf_op jit(solution)/shard_map/all_to_all | solution.py:75
  68.7 5.2 all-to-all-start.4
  73.9 3.2 copy.86
  77.1 23.2 %all-to-all-done.4 = bf16[128,8,1024]{2,0,1:T(8,128)(2,1)} async-done(((bf16[128,8,1024]{2,0,1:T(8,128)(2,1)}), bf16[128,8,1024]{2,0,1:T(8,128)(2,1)}, u32[]{:S(2)}, u32[]{:S(2)}) %all-to-all-start.4) | async-done | bytes 2097184 | tf_op jit(solution)/shard_map/all_to_all | solution.py:73
  100.3 5.2 all-to-all-start
  105.5 5.8 gather_fusion.2
  111.4 9.7 gather_fusion.6
  121.0 9.7 %gather_fusion.4 = bf16[1536,1024]{1,0:T(8,128)(2,1)} fusion(bf16[1024,1024]{1,0:T(8,128)(2,1)} %bitcast.16, s32[2048]{0:T(1024)S(1)} %pad_clamp_fusion), kind=kCustom, calls=%fused_computation.3.clone | custom fusion | bytes 6297600 | tf_op jit(solution)/shard_map/jit(_take)/gather | solution.py:83
  131.8 9.8 %gather_fusion = bf16[1536,1024]{1,0:T(8,128)(2,1)} fusion(bf16[1024,1024]{1,0:T(8,128)(2,1)} %bitcast.5, s32[2048]{0:T(1024)S(1)} %pad_clamp_fusion), kind=kCustom, calls=%fused_computation.clone | custom fusion | bytes 6297600 | tf_op jit(solution)/shard_map/jit(_take)/gather | solution.py:83
  141.6 7.2 select_select_fusion
  148.8 81.1 %all_to_all.217 = bf16[32,48,1024]{2,1,0:T(8,128)(2,1)} all-to-all(bf16[32,48,1024]{2,1,0:T(8,128)(2,1)S(1)} %bitcast.99), channel_id=1, replica_groups=mesh['seq'=32,'head'=8] {'seq'}, dimensions={0} | all-to-all | bytes 6291456 | tf_op jit(solution)/shard_map/all_to_all | solution.py:89
  230.0 76.3 %all_to_all.218 = bf16[32,48,1024]{2,1,0:T(8,128)(2,1)} all-to-all(bf16[32,48,1024]{2,1,0:T(8,128)(2,1)S(1)} %bitcast.98), channel_id=1, replica_groups=mesh['seq'=32,'head'=8] {'seq'}, dimensions={0} | all-to-all | bytes 6291456 | tf_op jit(solution)/shard_map/all_to_all | solution.py:90
  306.3 76.2 %all_to_all.219 = bf16[32,48,1024]{2,1,0:T(8,128)(2,1)} all-to-all(bf16[32,48,1024]{2,1,0:T(8,128)(2,1)S(1)} %bitcast.97), channel_id=1, replica_groups=mesh['seq'=32,'head'=8] {'seq'}, dimensions={0} | all-to-all | bytes 6291456 | tf_op jit(solution)/shard_map/all_to_all | solution.py:87
  382.6 7.7 all-to-all-start.5
  392.9 113.9 %all-reduce.1 = f32[64]{0:T(128)S(1)} all-reduce(f32[64]{0:T(128)S(1)} %select_reduce_fusion.3), channel_id=2, replica_groups=mesh['seq'=32,'head'=8] {'seq'}, use_global_device_ids=true, to_apply=%region_5.8.clone | all-reduce | flops 64 | bytes 512
  507.0 58.0 %all-reduce = f32[64]{0:T(128)S(1)} all-reduce(f32[64]{0:T(128)S(1)} %multiply_dynamic-update-slice_fusion), channel_id=1, replica_groups=mesh['seq'=32,'head'=8] {'seq'}, use_global_device_ids=true, to_apply=%add | all-reduce | flops 64 | bytes 512
  565.3 8.3 gather_fusion.3
  573.6 8.3 gather_fusion.7
  581.9 8.3 gather_fusion.1
  590.3 5.4 gather_fusion.5
  595.7 3.6 multiply_convert_fusion.1
  599.3 4.4 broadcast_select_fusion
  610.2 138.8 %while.20 = (s32[]{:T(128)}, bf16[1024,1024]{1,0:T(8,128)(2,1)}, f32[1024,1024]{1,0:T(8,128)}, f32[1024,1024]{1,0:T(8,128)}, bf16[1024,1024]{1,0:T(8,128)(2,1)},...) while((s32[]{:T(128)}, bf16[1024,1024]{1,0:T(8,128)(2,1)}, ...), condition=%wide.region_12.15_spmd.clone, body=%wide.region_8.14_spmd.clone.sunk | while | flops 1629221888 | bytes 68732144 | solution.py:168
  619.7 2.8 fusion.79
  749.0 3.2 copy.79
  753.2 3.9 scatter_custom_fusion.2
  757.1 6.8 all-to-all-start.10
  763.9 3.2 copy.80
  768.1 3.9 scatter_custom_fusion.4
  772.0 3.3 all-to-all-done.10
  775.4 5.9 all-to-all-start.12
  781.3 5.1 scatter_custom_fusion.3
  786.4 6.3 all-to-all-done.12
  792.7 36.4 %all-to-all-start.11 = ((bf16[8,128,128]{2,1,0:T(8,128)(2,1)}), bf16[8,128,128]{2,1,0:T(8,128)(2,1)S(1)}, u32[]{:S(2)}, u32[]{:S(2)}) async-start(bf16[8,128,128]{2,1,0:T(8,128)(2,1)} %bitcast.30), calls=%async_computation.11 | async-start | bytes 524288 | tf_op jit(solution)/shard_map/all_to_all | solution.py:203
  829.1 8.1 scatter_custom_fusion
  837.2 4.1 all-to-all-start.8
  841.3 5.4 scatter_custom_fusion.5
  846.7 66.4 %all-to-all-done.8 = bf16[32,48,1024]{2,1,0:T(8,128)(2,1)S(1)} async-done(((bf16[32,48,1024]{2,1,0:T(8,128)(2,1)}), bf16[32,48,1024]{2,1,0:T(8,128)(2,1)S(1)}, u32[]{:S(2)}, u32[]{:S(2)}) %all-to-all-start.8) | async-done | bytes 3145760 | tf_op jit(solution)/shard_map/all_to_all | solution.py:188
  913.1 6.9 all-to-all-start.13
  920.0 9.1 scatter_custom_fusion.1
  929.1 4.8 all-to-all-start.9
  936.9 23.2 %all-to-all-done.9 = bf16[8,128,1024]{2,1,0:T(8,128)(2,1)S(1)} async-done(((bf16[8,128,1024]{2,1,0:T(8,128)(2,1)}), bf16[8,128,1024]{2,1,0:T(8,128)(2,1)S(1)}, u32[]{:S(2)}, u32[]{:S(2)}) %all-to-all-start.9) | async-done | bytes 2097184 | tf_op jit(solution)/shard_map/all_to_all | solution.py:202
  962.5 4.1 copy.70
  (185 shorter events, 157.5 us)
Async XLA Ops:
  0.6 1.0 copy-start
  1.9 9.0 copy-start.8
  4.3 32.9 %all-to-all-start.2 = ((bf16[128,8,1024]{2,0,1:T(8,128)(2,1)}), bf16[128,8,1024]{2,0,1:T(8,128)(2,1)S(1)}, u32[]{:S(2)}, u32[]{:S(2)}) async-start(bf16[128,8,1024]{2,0,1:T(8,128)(2,1)} %all_to_all.161), calls=%async_computation.2 | async-start | bytes 4194304 | tf_op jit(solution)/shard_map/all_to_all | solution.py:74
  37.2 31.5 %all-to-all-start.6 = ((bf16[128,8,1024]{2,0,1:T(8,128)(2,1)}), bf16[128,8,1024]{2,0,1:T(8,128)(2,1)}, u32[]{:S(2)}, u32[]{:S(2)}) async-start(bf16[128,8,1024]{2,0,1:T(8,128)(2,1)} %all_to_all.175), calls=%async_computation.6 | async-start | bytes 4194304 | tf_op jit(solution)/shard_map/all_to_all | solution.py:75
  68.7 31.5 %all-to-all-start.4 = ((bf16[128,8,1024]{2,0,1:T(8,128)(2,1)}), bf16[128,8,1024]{2,0,1:T(8,128)(2,1)}, u32[]{:S(2)}, u32[]{:S(2)}) async-start(bf16[128,8,1024]{2,0,1:T(8,128)(2,1)} %bitcast.101), calls=%async_computation.4 | async-start | bytes 4194304 | tf_op jit(solution)/shard_map/all_to_all | solution.py:73
  77.1 28.4 %copy-start.10 = (s32[1,1536]{1,0:T(1,128)S(1)}, s32[1,1536]{1,0:T(1,128)}, u32[]{:S(2)}) copy-start(s32[1,1536]{1,0:T(1,128)} %param.21) | copy-start | bytes 18436
  100.3 31.5 %all-to-all-start = ((bf16[128,8,1024]{2,0,1:T(8,128)(2,1)}), bf16[128,8,1024]{2,0,1:T(8,128)(2,1)}, u32[]{:S(2)}, u32[]{:S(2)}) async-start(bf16[128,8,1024]{2,0,1:T(8,128)(2,1)} %bitcast.100), calls=%async_computation | async-start | bytes 4194304 | tf_op jit(solution)/shard_map/all_to_all | solution.py:72
  131.8 9.8 %copy-start.4 = (bf16[1536,1024]{1,0:T(8,128)(2,1)S(1)}, bf16[1536,1024]{1,0:T(8,128)(2,1)}, u32[]{:S(2)}) copy-start(bf16[1536,1024]{1,0:T(8,128)(2,1)} %gather_fusion.2) | copy-start | bytes 9437188
  382.5 7.8 copy-start.16
  382.5 8.0 copy-start.15
  382.5 9.9 %copy-start.12 = (f32[1024]{0:T(1024)S(1)}, f32[1024]{0:T(1024)}, u32[]{:S(2)}) copy-start(f32[1024]{0:T(1024)} %param.26) | copy-start | bytes 12292
  382.5 10.0 %copy-start.13 = (f32[1024]{0:T(1024)S(1)}, f32[1024]{0:T(1024)}, u32[]{:S(2)}) copy-start(f32[1024]{0:T(1024)} %param.27) | copy-start | bytes 12292
  382.5 10.0 %copy-start.14 = (s32[1024]{0:T(1024)S(1)}, s32[1024]{0:T(1024)}, u32[]{:S(2)}) copy-start(s32[1024]{0:T(1024)} %param.25) | copy-start | bytes 12292
  382.5 10.1 %copy-start.17 = (s32[128]{0:T(128)S(1)}, s32[128]{0:T(128)}, u32[]{:S(2)}) copy-start(s32[128]{0:T(128)} %param.24) | copy-start | bytes 1540
  382.5 182.7 %copy-start.9 = (s32[1,1024]{1,0:T(1,128)S(1)}, s32[1,1024]{1,0:T(1,128)}, u32[]{:S(2)}) copy-start(s32[1,1024]{1,0:T(1,128)} %param.22) | copy-start | bytes 12292
  382.6 207.7 %all-to-all-start.5 = ((bf16[32,48,1024]{2,1,0:T(8,128)(2,1)}), bf16[32,48,1024]{2,1,0:T(8,128)(2,1)S(1)}, u32[]{:S(2)}, u32[]{:S(2)}) async-start(bf16[32,48,1024]{2,1,0:T(8,128)(2,1)} %bitcast.96), calls=%async_computation.5 | async-start | bytes 6291456 | tf_op jit(solution)/shard_map/all_to_all | solution.py:88
  595.7 3.6 copy-start.5
  595.7 3.6 copy-start.6
  612.1 2.0 copy-start.2
  615.2 2.3 copy-start.3
  629.5 2.0 copy-start.2
  632.6 2.3 copy-start.3
  646.9 2.0 copy-start.2
  650.0 2.3 copy-start.3
  664.1 2.0 copy-start.2
  667.2 2.3 copy-start.3
  681.4 2.0 copy-start.2
  684.5 2.3 copy-start.3
  698.8 2.0 copy-start.2
  701.9 2.3 copy-start.3
  716.1 2.0 copy-start.2
  719.2 2.3 copy-start.3
  733.4 2.0 copy-start.2
  736.5 2.3 copy-start.3
  757.1 18.3 %all-to-all-start.10 = ((bf16[32,48,128]{2,1,0:T(8,128)(2,1)}), bf16[32,48,128]{2,1,0:T(8,128)(2,1)S(1)}, u32[]{:S(2)}, u32[]{:S(2)}) async-start(bf16[32,48,128]{2,1,0:T(8,128)(2,1)} %bitcast.28), calls=%async_computation.10 | async-start | bytes 786432 | tf_op jit(solution)/shard_map/all_to_all | solution.py:189
  767.1 14.2 %copy-start.11 = (s32[1,1536]{1,0:T(1,128)S(1)}, s32[1,1536]{1,0:T(1,128)}, u32[]{:S(2)}) copy-start(s32[1,1536]{1,0:T(1,128)} %param.21) | copy-start | bytes 18436
  775.4 17.3 %all-to-all-start.12 = ((bf16[32,48,128]{2,1,0:T(8,128)(2,1)}), bf16[32,48,128]{2,1,0:T(8,128)(2,1)S(1)}, u32[]{:S(2)}, u32[]{:S(2)}) async-start(bf16[32,48,128]{2,1,0:T(8,128)(2,1)} %bitcast.33), calls=%async_computation.12 | async-start | bytes 786432 | tf_op jit(solution)/shard_map/all_to_all | solution.py:190
  792.7 44.5 %copy-start.7 = (bf16[32,48,128]{2,1,0:T(8,128)(2,1)}, bf16[32,48,128]{2,1,0:T(8,128)(2,1)S(1)}, u32[]{:S(2)}) copy-start(bf16[32,48,128]{2,1,0:T(8,128)(2,1)S(1)} %all-to-all-done.12) | copy-start | bytes 1179652
  792.7 44.5 %all-to-all-start.11 = ((bf16[8,128,128]{2,1,0:T(8,128)(2,1)}), bf16[8,128,128]{2,1,0:T(8,128)(2,1)S(1)}, u32[]{:S(2)}, u32[]{:S(2)}) async-start(bf16[8,128,128]{2,1,0:T(8,128)(2,1)} %bitcast.30), calls=%async_computation.11 | async-start | bytes 524288 | tf_op jit(solution)/shard_map/all_to_all | solution.py:203
  837.2 75.9 %all-to-all-start.8 = ((bf16[32,48,1024]{2,1,0:T(8,128)(2,1)}), bf16[32,48,1024]{2,1,0:T(8,128)(2,1)S(1)}, u32[]{:S(2)}, u32[]{:S(2)}) async-start(bf16[32,48,1024]{2,1,0:T(8,128)(2,1)} %bitcast.23), calls=%async_computation.8 | async-start | bytes 6291456 | tf_op jit(solution)/shard_map/all_to_all | solution.py:188
  913.1 16.0 %all-to-all-start.13 = ((bf16[8,128,128]{2,1,0:T(8,128)(2,1)}), bf16[8,128,128]{2,1,0:T(8,128)(2,1)}, u32[]{:S(2)}, u32[]{:S(2)}) async-start(bf16[8,128,128]{2,1,0:T(8,128)(2,1)} %bitcast.107), calls=%async_computation.13 | async-start | bytes 524288 | tf_op jit(solution)/shard_map/all_to_all | solution.py:204
  929.1 31.0 %all-to-all-start.9 = ((bf16[8,128,1024]{2,1,0:T(8,128)(2,1)}), bf16[8,128,1024]{2,1,0:T(8,128)(2,1)S(1)}, u32[]{:S(2)}, u32[]{:S(2)}) async-start(bf16[8,128,1024]{2,1,0:T(8,128)(2,1)} %bitcast.25), calls=%async_computation.9 | async-start | bytes 4194304 | tf_op jit(solution)/shard_map/all_to_all | solution.py:202
  960.1 6.4 copy-start.1
where the time goes:
time: 978 us; the launch traced here: 967 us
  blocking collectives  406 us (42%)
  waiting for transfers between devices  167 us (17%)
  local copies, waits for them, and re-layouts  151 us (15%)
  matrix products  108 us (11%)
  starting transfers between devices  94.9 us (10%)
  other arithmetic  36.9 us (4%)
    unnamed x2, blocking collectives  172 us
    all_to_all x1, blocking collectives, body(): lax.all_to_all(pack_rows(key_group), 'seq', split_axis=0, concat_axis=0,...  81.1 us
    all_to_all x1, blocking collectives, body(): lax.all_to_all(pack_rows(value_group), 'seq', split_axis=0, concat_axis=0...  76.3 us
    all_to_all x1, blocking collectives, body(): lax.all_to_all(pack_rows(query_group), 'seq', split_axis=0, concat_axis=0...  76.2 us
    all_to_all x1, waiting for transfers between devices, body(): lax.all_to_all(spread_rows(grad_query), 'seq', split_axis=0, concat_axis=...  66.4 us
    all_to_all x1, starting transfers between devices, body(): lax.all_to_all(place_rows(returned[1]), 'head', split_axis=0, concat_axis...  36.4 us
    gather x4, local copies, waits for them, and re-layouts, pack_rows(): jnp.take(block, safe_rows, axis=0)  35 us
    all_to_all x1, waiting for transfers between devices, body(): lax.all_to_all(value_send, 'head', split_axis=1, concat_axis=0, tiled=True)  23.2 us
  transfers between devices with their start and end apart: 11, of which 8 were waited for; matrix products, arithmetic and copies ran while one was open for 10% of the time, Pallas kernels for 0%

commit v1 on v0

v1 whole, which is shorter than its diff:
```python
import math

import jax
import jax.numpy as jnp
from jax import lax
from jax.experimental import pallas as pl
from jax.experimental.pallas import tpu as pltpu
from jax.sharding import Mesh
from jax.sharding import PartitionSpec as P

D = 128
CAP = 48
KB = 128
NZ = 8
NY = 4
NH = 8
BETA = 0.1
BF = jnp.bfloat16
F32 = jnp.float32


def dot(a, b, ca, cb):
    return lax.dot_general(a, b, (((ca,), (cb,)), ((), ())), preferred_element_type=F32)


def attention_kernel(
    rng, q_ref, u_ref, kv_ref, p_ref, st_ref, c_ref, gq_ref, gkv_ref, s_scr, dp_scr, kt_scr, dq_acc, gk_acc, gv_acc
):
    owner = pl.program_id(0)
    heads = q_ref.shape[3] // D
    lanes = heads * CAP
    scale = 1.0 / math.sqrt(D)
    kt_scr[...] = kv_ref[0, :, :D].astype(F32).T.astype(BF)
    gk_acc[...] = jnp.zeros_like(gk_acc)
    gv_acc[...] = jnp.zeros_like(gv_acc)

    def stack(block):
        return jnp.concatenate([block[:, h * D : (h + 1) * D] for h in range(heads)], axis=0)

    def fold(x, op):
        return op(x.reshape(KB // 8, 8, lanes), axis=0)

    for y in range(NY):
        q = stack(q_ref[y, 0])
        coef = c_ref[0, y * CAP : (y + 1) * CAP, :]
        g = stack((u_ref[y, 0].astype(F32) * coef).astype(BF))
        pos = p_ref[0, y : y + 1, :]
        start = st_ref[0, y : y + 1, :]
        lo = rng[0, owner * NY + y]
        hi = rng[1, owner * NY + y]

        def score_pass(j, top):
            ks = pl.multiple_of(j * KB, KB)
            s = dot(kv_ref[0, pl.ds(ks, KB), :D], q, 1, 1) * scale
            key = lax.broadcasted_iota(jnp.int32, (KB, lanes), 0) + ks
            s = jnp.where((key >= start) & (key <= pos), s, -1e30)
            s_scr[pl.ds(ks, KB), :] = s
            return jnp.maximum(top, fold(s, jnp.max))

        top = lax.fori_loop(lo, hi, score_pass, jnp.full((8, lanes), -1e30, F32))
        top = jnp.max(top, axis=0, keepdims=True)

        def weigh_pass(j, sums):
            total, cross = sums
            ks = pl.multiple_of(j * KB, KB)
            e = jnp.exp(s_scr[pl.ds(ks, KB), :] - top)
            dp = dot(kv_ref[0, pl.ds(ks, KB), D:], g, 1, 1)
            s_scr[pl.ds(ks, KB), :] = e
            dp_scr[pl.ds(ks, KB), :] = dp
            return (total + fold(e, jnp.sum), cross + fold(e * dp, jnp.sum))

        zero = jnp.zeros((8, lanes), F32)
        total, cross = lax.fori_loop(lo, hi, weigh_pass, (zero, zero))
        inverse = 1.0 / jnp.sum(total, axis=0, keepdims=True)
        row_dot = jnp.sum(cross, axis=0, keepdims=True) * inverse
        dq_acc[...] = jnp.zeros_like(dq_acc)

        def grad_pass(j, carry):
            ks = pl.multiple_of(j * KB, KB)
            probs = s_scr[pl.ds(ks, KB), :] * inverse
            gs = (probs * (dp_scr[pl.ds(ks, KB), :] - row_dot) * scale).astype(BF)
            gv_acc[pl.ds(ks, KB), :] += dot(probs.astype(BF), g, 1, 0)
            gk_acc[pl.ds(ks, KB), :] += dot(gs, q, 1, 0)
            dq_acc[...] += dot(kt_scr[:, pl.ds(ks, KB)], gs, 1, 0)
            return carry

        lax.fori_loop(lo, hi, grad_pass, 0)
        gq = dq_acc[...].T.astype(BF)
        for h in range(heads):
            gq_ref[y, 0, :, h * D : (h + 1) * D] = gq[h * CAP : (h + 1) * CAP, :]
    gkv_ref[0, :, :D] = gk_acc[...].astype(BF)
    gkv_ref[0, :, D:] = gv_acc[...].astype(BF)


def attention(rng, q, u, kv, pos, start, coef):
    rows = kv.shape[1]
    width = q.shape[3]
    lanes = (width // D) * CAP
    slot = pl.BlockSpec((NY, 1, CAP, width), lambda i, r: (0, i, 0, 0))
    pair = pl.BlockSpec((1, rows, 2 * D), lambda i, r: (i, 0, 0))
    lane = pl.BlockSpec((1, NY, lanes), lambda i, r: (i, 0, 0))
    return pl.pallas_call(
        attention_kernel,
        grid_spec=pltpu.PrefetchScalarGridSpec(
            num_scalar_prefetch=1,
            grid=(NZ,),
            in_specs=[slot, slot, pair, lane, lane, pl.BlockSpec((1, NY * CAP, 1), lambda i, r: (i, 0, 0))],
            out_specs=[slot, pair],
            scratch_shapes=[
                pltpu.VMEM((rows, lanes), F32),
                pltpu.VMEM((rows, lanes), F32),
                pltpu.VMEM((D, rows), BF),
                pltpu.VMEM((D, lanes), F32),
                pltpu.VMEM((rows, D), F32),
                pltpu.VMEM((rows, D), F32),
            ],
        ),
        out_shape=[jax.ShapeDtypeStruct(q.shape, BF), jax.ShapeDtypeStruct(kv.shape, BF)],
        name="owner_attention",
    )(rng, q, u, kv, pos, start, coef)


def pick(index, count, rows):
    hot = index[:, None] == jnp.arange(count, dtype=jnp.int32)[None, :]
    return dot(hot.astype(BF), rows, 1, 0).astype(BF)


def place(index, count, rows):
    hot = jnp.arange(count, dtype=jnp.int32)[:, None] == index[None, :]
    return dot(hot.astype(BF), rows, 1, 0).astype(BF)


def body(
    queries, keys, values, upstream, send_rows, recv_rows, doc_lengths, pair_docs, response_mask, policy_logp, ref_logp
):
    tok = queries.shape[0]
    rows = tok * NH
    width = queries.shape[1] // NH
    seq = ("z", "y")
    slots = send_rows.shape[1]
    my_y = lax.axis_index("y")
    send = send_rows[0]
    send_y = send.reshape(NZ, NY, CAP).transpose(1, 0, 2).reshape(slots)
    recv = recv_rows[0]

    with jax.named_scope("kv_in"):
        kv = jnp.concatenate([keys.reshape(tok, NH, D), values.reshape(tok, NH, D)], axis=2).transpose(1, 0, 2)
        kv = lax.all_to_all(kv, "head", 0, 0).reshape(rows, 2 * D)
        kv = pick(send, rows, kv).reshape(NZ * NY, CAP, 2 * D)
        kv = lax.all_to_all(kv, seq, 0, 0).reshape(slots, 2 * D)
        kv = pick(recv, slots, kv)
        kv = lax.all_gather(kv, "z", axis=0)

    with jax.named_scope("meta"):
        place_of = jnp.arange(rows, dtype=jnp.int32)
        slot_id = jnp.arange(slots, dtype=jnp.int32)
        pos = jnp.sum(jnp.where(recv[None, :] == slot_id[:, None], place_of[None, :] + 1, 0), axis=1) - 1
        ends = jnp.cumsum(doc_lengths[0])
        doc_row = jnp.sum((place_of[:, None] >= ends[None, :]).astype(jnp.int32), axis=1)
        member = doc_row[:, None] == jnp.arange(4, dtype=jnp.int32)[None, :]
        gap_row = response_mask.astype(F32) * (policy_logp - ref_logp)
        gap = jnp.sum(jnp.where(member, gap_row[:, None], 0.0), axis=0)
        part = jnp.broadcast_to(pos.astype(F32).reshape(NZ, 1, NY * CAP), (NZ, NY, NY * CAP)).reshape(NZ * NY, NY * CAP)
        small = jnp.broadcast_to(
            jnp.concatenate([gap, ends.astype(F32), jnp.zeros((56,), F32)])[None, :], (NZ * NY, 64)
        )
        got = lax.all_to_all(jnp.concatenate([part, small], axis=1), seq, 0, 0)
        gaps = got[:, 192:196].reshape(128)
        mine = lax.dynamic_index_in_dim(got.reshape(NZ, NY, 256), my_y, 1, keepdims=False)
        other = pair_docs.reshape(64, 2)[:, ::-1].reshape(128)
        doc_id = jnp.arange(128, dtype=jnp.int32)
        own_hot = pair_docs[:, None] == doc_id[None, :]
        sign = 1.0 - 2.0 * (doc_id % 2).astype(F32)
        own_gap = jnp.sum(jnp.where(own_hot, gaps[None, :], 0.0), axis=1)
        other_gap = jnp.sum(jnp.where(other[:, None] == doc_id[None, :], gaps[None, :], 0.0), axis=1)
        margin = BETA * (own_gap - other_gap) * sign
        weight = -sign * (BETA * jax.nn.sigmoid(-margin))
        doc_coef = jnp.sum(jnp.where(own_hot, weight[:, None], 0.0), axis=0)
        my_coef = lax.dynamic_index_in_dim(doc_coef.reshape(NZ, NY, 4), my_y, 1, keepdims=False)
        q_pos = mine[:, :192].astype(jnp.int32)
        q_ends = mine[:, 196:200].astype(jnp.int32)
        past = q_pos[:, :, None] >= q_ends[:, None, :]
        q_doc = jnp.sum(past.astype(jnp.int32), axis=2)
        q_start = jnp.max(jnp.where(past, q_ends[:, None, :], 0), axis=2)
        in_doc = (q_doc[:, :, None] == jnp.arange(4, dtype=jnp.int32)) & (q_pos[:, :, None] >= 0)
        coef = jnp.sum(jnp.where(in_doc, my_coef[:, None, :], 0.0), axis=2)
        q_pos = q_pos.reshape(NZ, NY, CAP)
        q_start = q_start.reshape(NZ, NY, CAP)
        last = jnp.max(q_pos, axis=2) // KB + 1
        first = jnp.min(jnp.where(q_pos >= 0, q_start, rows), axis=2) // KB
        last = jnp.clip(last, 0, rows // KB)
        first = jnp.clip(first, 0, last)
        rng = jnp.stack([first.reshape(-1), last.reshape(-1)])
        heads = width // D
        pos_lane = jnp.tile(q_pos, (1, 1, heads))
        start_lane = jnp.tile(q_start, (1, 1, heads))

    def move_in(x):
        x = x.reshape(tok, NH, width).transpose(1, 0, 2)
        x = lax.all_to_all(x, "head", 0, 0).reshape(rows, width)
        x = pick(send_y, rows, x).reshape(NY, slots // NY, width)
        return lax.all_to_all(x, "y", 0, 0).reshape(NY, NZ, CAP, width)

    with jax.named_scope("q_in"):
        q = move_in(queries)
    with jax.named_scope("u_in"):
        u = move_in(upstream)

    gq, gkv = attention(rng, q, u, kv, pos_lane, start_lane, coef[:, :, None])

    with jax.named_scope("kv_out"):
        gkv = lax.psum_scatter(gkv, "z", scatter_dimension=0)
        gkv = pick(pos, rows, gkv).reshape(NZ * NY, CAP, 2 * D)
        gkv = lax.all_to_all(gkv, seq, 0, 0).reshape(slots, 2 * D)
        gkv = place(send, rows, gkv).reshape(NH, tok, 2 * D)
        gkv = lax.all_to_all(gkv, "head", 0, 0).transpose(1, 0, 2)
        gk = gkv[:, :, :D].reshape(tok, NH * D)
        gv = gkv[:, :, D:].reshape(tok, NH * D)
    with jax.named_scope("q_out"):
        gq = lax.all_to_all(gq.reshape(NY, slots // NY, width), "y", 0, 0).reshape(slots, width)
        gq = place(send_y, rows, gq).reshape(NH, tok, width)
        gq = lax.all_to_all(gq, "head", 0, 0).transpose(1, 0, 2).reshape(tok, NH * width)
    return (gq, gk, gv)


def solution(mesh):
    grid = Mesh(mesh.devices.reshape(NZ, NY, NH), ("z", "y", "head"))
    tokens = P(("z", "y", "head"), None)
    group = P(("z", "y"), None)
    line = P(("z", "y"))
    return jax.shard_map(
        body,
        mesh=grid,
        in_specs=(tokens, tokens, tokens, tokens, group, group, group, P(), line, line, line),
        out_specs=(tokens, tokens, tokens),
        check_vma=False,
    )
```

time: 978 us -> 423 us (0.43); the launches traced: 967 us -> 423 us
  blocking collectives: 406 us -> 0 us
  local copies, waits for them, and re-layouts: 151 us -> 24.6 us
  matrix products: 108 us -> 28.2 us
  Pallas kernels: 0 us -> 65.3 us
  waiting for transfers between devices: 167 us -> 223 us
  other arithmetic: 36.9 us -> 3.58 us
  starting transfers between devices: 94.9 us -> 64.6 us
  between operations: 2.71 us -> 14.4 us
    all_to_all x3 -> x0, blocking collectives: 234 us -> none  [the longest x1 81.1 us: body(): lax.all_to_all(pack_rows(key_group), 'seq', split_axis=0, concat_axis=0,...]
    unnamed x2 -> x0, blocking collectives: 172 us -> none
    dot_general x48 -> x7, matrix products: 108 us -> 28.2 us  [dot(): lax.dot_general(a, b, (((ca,), (cb,)), ((), ())), preferred_element_type=...]
    gather x8 -> x0, local copies, waits for them, and re-layouts: 65.3 us -> none  [the longest x4 35 us: pack_rows(): jnp.take(block, safe_rows, axis=0)]
    pallas_call x0 -> x1, Pallas kernels: none -> 65.3 us  [attention(): pl.pallas_call(attention_kernel, grid_spec=pltpu.PrefetchScalarGridSpec(n...]
    reduce_scatter x0 -> x1, waiting for transfers between devices: none -> 51.3 us  [body(): gkv = lax.psum_scatter(gkv, 'z', scatter_dimension=0)]
    all_to_all x11, starting transfers between devices: 94.9 us -> 64.3 us  [the longest x2 12.7 us: move_in(): x = lax.all_to_all(x, 'head', 0, 0).reshape(rows, width)]
    scatter x4 -> x0, local copies, waits for them, and re-layouts: 27.7 us -> none  [the longest x3 19.6 us: place_rows(): return jnp.zeros((group_rows, block.shape[1]), block.dtype).at[target_row...]
  transfers between devices with their start and end apart: 11 -> 13, of which waited for: 8 -> 11; matrix products, arithmetic and copies ran while one was open for 10% -> 12% of each run, Pallas kernels for 0% -> 0%
where the time goes in v1:
time: 423 us
  waiting for transfers between devices  223 us (53%)
  Pallas kernels  65.3 us (15%)
  starting transfers between devices  64.6 us (15%)
  matrix products  28.2 us (7%)
  local copies, waits for them, and re-layouts  24.6 us (6%)
  between operations  14.4 us (3%)
    pallas_call x1, Pallas kernels, attention(): pl.pallas_call(attention_kernel, grid_spec=pltpu.PrefetchScalarGridSpec(n...  65.3 us
    all_to_all x2, waiting for transfers between devices, move_in(): return lax.all_to_all(x, 'y', 0, 0).reshape(NY, NZ, CAP, width)  55.8 us
    reduce_scatter x1, waiting for transfers between devices, body(): gkv = lax.psum_scatter(gkv, 'z', scatter_dimension=0)  51.3 us
    all_to_all x2, waiting for transfers between devices, move_in(): x = lax.all_to_all(x, 'head', 0, 0).reshape(rows, width)  37.2 us
    dot_general x7, matrix products, dot(): lax.dot_general(a, b, (((ca,), (cb,)), ((), ())), preferred_element_type=...  28.2 us
    all_to_all x1, waiting for transfers between devices, body(): lax.all_to_all(gq, 'head', 0, 0).transpose(1, 0, 2).reshape(tok, NH * width)  23.2 us
    all_to_all x1, waiting for transfers between devices, body(): kv = lax.all_to_all(kv, seq, 0, 0).reshape(slots, 2 * D)  17.3 us
    all_to_all x1, waiting for transfers between devices, body(): gkv = lax.all_to_all(gkv, seq, 0, 0).reshape(slots, 2 * D)  16.5 us
  transfers between devices with their start and end apart: 13, of which 11 were waited for; matrix products, arithmetic and copies ran while one was open for 12% of the time, Pallas kernels for 0%

profile of v1, /device:TPU:1, one launch (start us, length us, event | category | flops | bytes accessed | tf_op | source)
XLA Modules:
  0.0 423.2 jit_solution(4769308861582818313)
XLA Ops:
  7.2 1.2 copy.60
  8.4 1.1 copy.61
  9.5 0.8 maximum_bitcast_fusion
  10.3 6.6 %all-to-all-start.5 = ((bf16[8,128,256]{1,2,0:T(8,128)(2,1)}), bf16[8,128,256]{1,2,0:T(8,128)(2,1)S(1)}, u32[]{:S(2)}, u32[]{:S(2)}) async-start(bf16[8,128,256]{1,2,0:T(8,128)(2,1)} %maximum_bitcast_fusion), calls=%async_computation.5 | async-start | bytes 1048576 | tf_op jit(solution)/shard_map/kv_in/all_to_all | solution.py:148
  17.1 0.7 select_reduce_fusion
  18.4 0.6 all_to_all.38
  19.0 7.3 %all-to-all-done.5 = bf16[8,128,256]{1,2,0:T(8,128)(2,1)S(1)} async-done(((bf16[8,128,256]{1,2,0:T(8,128)(2,1)}), bf16[8,128,256]{1,2,0:T(8,128)(2,1)S(1)}, u32[]{:S(2)}, u32[]{:S(2)}) %all-to-all-start.5) | async-done | bytes 524320 | tf_op jit(solution)/shard_map/kv_in/all_to_all | solution.py:148
  26.3 10.4 %all-to-all-start = ((f32[32,1,256]{2,1,0:T(1,128)}), f32[32,1,256]{2,1,0:T(1,128)S(1)}, u32[]{:S(2)}, u32[]{:S(2)}) async-start(f32[32,1,256]{2,1,0:T(1,128)} %all_to_all.38), calls=%async_computation | async-start | bytes 65536 | tf_op jit(solution)/shard_map/meta/all_to_all | solution.py:167
  36.9 2.1 fusion.17
  39.1 6.4 %all-to-all-done = f32[32,1,256]{2,1,0:T(1,128)S(1)} async-done(((f32[32,1,256]{2,1,0:T(1,128)}), f32[32,1,256]{2,1,0:T(1,128)S(1)}, u32[]{:S(2)}, u32[]{:S(2)}) %all-to-all-start) | async-done | bytes 32800 | tf_op jit(solution)/shard_map/meta/all_to_all | solution.py:167
  45.5 3.9 all-to-all-start.6
  49.4 2.4 copy.56
  51.8 17.3 %all-to-all-done.6 = bf16[32,48,256]{2,1,0:T(8,128)(2,1)S(1)} async-done(((bf16[32,48,256]{2,1,0:T(8,128)(2,1)}), bf16[32,48,256]{2,1,0:T(8,128)(2,1)S(1)}, u32[]{:S(2)}, u32[]{:S(2)}) %all-to-all-start.6) | async-done | bytes 786464 | tf_op jit(solution)/shard_map/kv_in/all_to_all | solution.py:150
  69.1 7.5 %all-to-all-start.1 = ((bf16[8,128,1024]{1,2,0:T(8,128)(2,1)}), bf16[8,128,1024]{1,2,0:T(8,128)(2,1)S(1)}, u32[]{:S(2)}, u32[]{:S(2)}) async-start(bf16[8,128,1024]{1,2,0:T(8,128)(2,1)} %bitcast.67), calls=%async_computation.1 | async-start | bytes 4194304 | tf_op jit(solution)/shard_map/q_in/all_to_all | solution.py:200
  76.6 1.9 fusion.20
  78.6 4.1 copy.58
  82.7 20.2 %all-to-all-done.1 = bf16[8,128,1024]{1,2,0:T(8,128)(2,1)S(1)} async-done(((bf16[8,128,1024]{1,2,0:T(8,128)(2,1)}), bf16[8,128,1024]{1,2,0:T(8,128)(2,1)S(1)}, u32[]{:S(2)}, u32[]{:S(2)}) %all-to-all-start.1) | async-done | bytes 2097184 | tf_op jit(solution)/shard_map/q_in/all_to_all | solution.py:200
  102.9 5.2 %all-to-all-start.3 = ((bf16[8,128,1024]{1,2,0:T(8,128)(2,1)}), bf16[8,128,1024]{1,2,0:T(8,128)(2,1)}, u32[]{:S(2)}, u32[]{:S(2)}) async-start(bf16[8,128,1024]{1,2,0:T(8,128)(2,1)} %bitcast.68), calls=%async_computation.3 | async-start | bytes 4194304 | tf_op jit(solution)/shard_map/u_in/all_to_all | solution.py:200
  108.2 2.6 copy.57
  110.8 6.6 %fusion.7 = bf16[1536,1024]{1,0:T(8,128)(2,1)} fusion(bf16[1024,1024]{1,0:T(8,128)(2,1)} %bitcast.76, s32[1536]{0:T(1024)S(1)} %eq.77), kind=kOutput, calls=%fused_computation.15 | convolution fusion | flops 3224371200 | bytes 5249024 | tf_op jit(solution)/shard_map/q_in/dot_general | solution.py:23
  117.4 17.0 %all-to-all-done.3 = bf16[8,128,1024]{1,2,0:T(8,128)(2,1)} async-done(((bf16[8,128,1024]{1,2,0:T(8,128)(2,1)}), bf16[8,128,1024]{1,2,0:T(8,128)(2,1)}, u32[]{:S(2)}, u32[]{:S(2)}) %all-to-all-start.3) | async-done | bytes 2097184 | tf_op jit(solution)/shard_map/u_in/all_to_all | solution.py:200
  134.4 3.9 all-to-all-start.2
  138.3 3.9 copy.59
  142.2 6.6 %fusion.8 = bf16[1536,1024]{1,0:T(8,128)(2,1)} fusion(bf16[1024,1024]{1,0:T(8,128)(2,1)} %bitcast.77, s32[1536]{0:T(1024)S(1)} %eq.77), kind=kOutput, calls=%fused_computation.16 | convolution fusion | flops 3224371200 | bytes 5249024 | tf_op jit(solution)/shard_map/u_in/dot_general | solution.py:23
  148.8 25.9 %all-to-all-done.2 = bf16[4,384,1024]{2,1,0:T(8,128)(2,1)S(1)} async-done(((bf16[4,384,1024]{2,1,0:T(8,128)(2,1)}), bf16[4,384,1024]{2,1,0:T(8,128)(2,1)S(1)}, u32[]{:S(2)}, u32[]{:S(2)}) %all-to-all-start.2) | async-done | bytes 3145760 | tf_op jit(solution)/shard_map/q_in/all_to_all | solution.py:202
  174.7 1.7 copy-done
  176.5 4.6 %all-to-all-start.4 = ((bf16[4,384,1024]{2,1,0:T(8,128)(2,1)}), bf16[4,384,1024]{2,1,0:T(8,128)(2,1)}, u32[]{:S(2)}, u32[]{:S(2)}) async-start(bf16[4,384,1024]{2,1,0:T(8,128)(2,1)} %bitcast.71), calls=%async_computation.4 | async-start | bytes 6291456 | tf_op jit(solution)/shard_map/u_in/all_to_all | solution.py:202
  181.1 0.2 reduce-scatter.2.cloned.1.call-start
  182.5 0.4 select_reduce_fusion.5
  183.6 0.7 tile.17.p_ref
  184.3 0.7 tile.19.st_ref
  185.1 1.2 copy.64.c_ref
  186.3 0.5 pad_add_fusion.rng
  186.8 29.9 %all-to-all-done.4 = bf16[4,384,1024]{2,1,0:T(8,128)(2,1)} async-done(((bf16[4,384,1024]{2,1,0:T(8,128)(2,1)}), bf16[4,384,1024]{2,1,0:T(8,128)(2,1)}, u32[]{:S(2)}, u32[]{:S(2)}) %all-to-all-start.4) | async-done | bytes 3145760 | tf_op jit(solution)/shard_map/u_in/all_to_all | solution.py:202
  216.7 65.3 %owner_attention.1 = (bf16[4,8,48,1024]{3,2,1,0:T(8,128)(2,1)}, bf16[8,1024,256]{2,1,0:T(8,128)(2,1)}) custom-call(s32[2,32]{1,0:T(2,128)} %pad_add_fusion.rng, bf16[4,8,48,1024]{3,2,1,0:T(8,128)(2,1)} %bitcast.66, bf16[4,8,48,1024]{3,2,1,0:T(8,128)(2,1)} %bitcast.13.u_ref, bf16[8,1024,256]{2,1,0:T(8,128)(2,1)} %bitcast.70, s32[8,4,384]{2,1,0:T(4,128)} %tile.17.p_ref, ...), custom_call_target="tpu_custom_call" | custom-call | tf_op jit(solution)/shard_map/owner_attention/pallas_call | solution.py:102
  282.0 3.7 all-to-all-start.7
  285.7 51.3 %reduce-scatter.2.cloned.1.call-done = bf16[1,1024,256]{2,1,0:T(8,128)(2,1)} async-done(((bf16[8,1024,256]{2,1,0:T(8,128)(2,1)}), bf16[1,1024,256]{2,1,0:T(8,128)(2,1)}) %reduce-scatter.2.cloned.1.call-update) | async-done | bytes 524304 | tf_op jit(solution)/shard_map/kv_out/reduce_scatter | solution.py:212
  337.1 3.2 fusion.16
  340.3 7.0 %all-to-all-start.9 = ((bf16[32,48,256]{2,1,0:T(8,128)(2,1)}), bf16[32,48,256]{2,1,0:T(8,128)(2,1)}, u32[]{:S(2)}, u32[]{:S(2)}) async-start(bf16[32,48,256]{2,1,0:T(8,128)(2,1)} %bitcast.82), calls=%async_computation.10 | async-start | bytes 1572864 | tf_op jit(solution)/shard_map/kv_out/all_to_all | solution.py:214
  347.3 4.6 %fusion.18 = bf16[1024,1024]{1,0:T(8,128)(2,1)} fusion(bf16[1536,1024]{1,0:T(8,128)(2,1)S(1)} %bitcast.72, s32[1536]{0:T(1024)S(1)} %eq.77), kind=kOutput, calls=%fused_computation.26 | convolution fusion | flops 3223846912 | bytes 5249024 | tf_op jit(solution)/shard_map/q_out/dot_general | solution.py:23
  351.9 16.5 %all-to-all-done.9 = bf16[32,48,256]{2,1,0:T(8,128)(2,1)} async-done(((bf16[32,48,256]{2,1,0:T(8,128)(2,1)}), bf16[32,48,256]{2,1,0:T(8,128)(2,1)}, u32[]{:S(2)}, u32[]{:S(2)}) %all-to-all-start.9) | async-done | bytes 786464 | tf_op jit(solution)/shard_map/kv_out/all_to_all | solution.py:214
  368.3 7.1 %all-to-all-start.8 = ((bf16[8,128,1024]{2,1,0:T(8,128)(2,1)}), bf16[8,128,1024]{2,1,0:T(8,128)(2,1)S(1)}, u32[]{:S(2)}, u32[]{:S(2)}) async-start(bf16[8,128,1024]{2,1,0:T(8,128)(2,1)} %bitcast.75), calls=%async_computation.8 | async-start | bytes 4194304 | tf_op jit(solution)/shard_map/q_out/all_to_all | solution.py:222
  375.4 3.0 fusion.19
  378.5 23.2 %all-to-all-done.8 = bf16[8,128,1024]{2,1,0:T(8,128)(2,1)S(1)} async-done(((bf16[8,128,1024]{2,1,0:T(8,128)(2,1)}), bf16[8,128,1024]{2,1,0:T(8,128)(2,1)S(1)}, u32[]{:S(2)}, u32[]{:S(2)}) %all-to-all-start.8) | async-done | bytes 2097184 | tf_op jit(solution)/shard_map/q_out/all_to_all | solution.py:222
  401.6 4.4 %all-to-all-start.10 = ((bf16[8,128,256]{2,1,0:T(8,128)(2,1)}), bf16[8,128,256]{2,1,0:T(8,128)(2,1)S(1)}, u32[]{:S(2)}, u32[]{:S(2)}) async-start(bf16[8,128,256]{2,1,0:T(8,128)(2,1)} %bitcast.30), calls=%async_computation.11 | async-start | bytes 1048576 | tf_op jit(solution)/shard_map/kv_out/all_to_all | solution.py:216
  406.0 1.6 copy.71
  407.5 7.8 %all-to-all-done.10 = bf16[8,128,256]{2,1,0:T(8,128)(2,1)S(1)} async-done(((bf16[8,128,256]{2,1,0:T(8,128)(2,1)}), bf16[8,128,256]{2,1,0:T(8,128)(2,1)S(1)}, u32[]{:S(2)}, u32[]{:S(2)}) %all-to-all-start.10) | async-done | bytes 524320 | tf_op jit(solution)/shard_map/kv_out/all_to_all | solution.py:216
  415.5 0.9 copy_bitcast_fusion
  (70 shorter events, 3.0 us)
Async XLA Ops:
  7.2 9.8 %copy-start.8 = (s32[1,4]{1,0:T(1,128)S(1)}, s32[1,4]{1,0:T(1,128)}, u32[]{:S(2)}) copy-start(s32[1,4]{1,0:T(1,128)} %param.17) | copy-start | bytes 52
  7.2 10.0 %copy-start.7 = (s32[1,1024]{1,0:T(1,128)S(1)}, s32[1,1024]{1,0:T(1,128)}, u32[]{:S(2)}) copy-start(s32[1,1024]{1,0:T(1,128)} %param.16) | copy-start | bytes 12292
  7.2 10.7 %copy-start.4 = (f32[1024]{0:T(1024)S(1)}, f32[1024]{0:T(1024)}, u32[]{:S(2)}) copy-start(f32[1024]{0:T(1024)} %param.21) | copy-start | bytes 12292
  7.2 10.7 %copy-start.3 = (f32[1024]{0:T(1024)S(1)}, f32[1024]{0:T(1024)}, u32[]{:S(2)}) copy-start(f32[1024]{0:T(1024)} %param.20) | copy-start | bytes 12292
  7.2 10.7 %copy-start.5 = (s32[1024]{0:T(1024)S(1)}, s32[1024]{0:T(1024)}, u32[]{:S(2)}) copy-start(s32[1024]{0:T(1024)} %param.19) | copy-start | bytes 12292
  7.2 10.8 %copy-start.2 = (s32[1,1536]{1,0:T(1,128)S(1)}, s32[1,1536]{1,0:T(1,128)}, u32[]{:S(2)}) copy-start(s32[1,1536]{1,0:T(1,128)} %param.15) | copy-start | bytes 18436
  10.3 16.0 %all-to-all-start.5 = ((bf16[8,128,256]{1,2,0:T(8,128)(2,1)}), bf16[8,128,256]{1,2,0:T(8,128)(2,1)S(1)}, u32[]{:S(2)}, u32[]{:S(2)}) async-start(bf16[8,128,256]{1,2,0:T(8,128)(2,1)} %maximum_bitcast_fusion), calls=%async_computation.5 | async-start | bytes 1048576 | tf_op jit(solution)/shard_map/kv_in/all_to_all | solution.py:148
  26.3 19.1 %all-to-all-start = ((f32[32,1,256]{2,1,0:T(1,128)}), f32[32,1,256]{2,1,0:T(1,128)S(1)}, u32[]{:S(2)}, u32[]{:S(2)}) async-start(f32[32,1,256]{2,1,0:T(1,128)} %all_to_all.38), calls=%async_computation | async-start | bytes 65536 | tf_op jit(solution)/shard_map/meta/all_to_all | solution.py:167
  36.9 12.5 %copy-start.1 = (bf16[128,8192]{1,0:T(8,128)(2,1)S(1)}, bf16[128,8192]{1,0:T(8,128)(2,1)}, u32[]{:S(2)}) copy-start(bf16[128,8192]{1,0:T(8,128)(2,1)} %param.11) | copy-start | bytes 6291460
  45.5 23.6 %all-to-all-start.6 = ((bf16[32,48,256]{2,1,0:T(8,128)(2,1)}), bf16[32,48,256]{2,1,0:T(8,128)(2,1)S(1)}, u32[]{:S(2)}, u32[]{:S(2)}) async-start(bf16[32,48,256]{2,1,0:T(8,128)(2,1)} %bitcast.83), calls=%async_computation.6 | async-start | bytes 1572864 | tf_op jit(solution)/shard_map/kv_in/all_to_all | solution.py:150
  69.1 33.8 %all-to-all-start.1 = ((bf16[8,128,1024]{1,2,0:T(8,128)(2,1)}), bf16[8,128,1024]{1,2,0:T(8,128)(2,1)S(1)}, u32[]{:S(2)}, u32[]{:S(2)}) async-start(bf16[8,128,1024]{1,2,0:T(8,128)(2,1)} %bitcast.67), calls=%async_computation.1 | async-start | bytes 4194304 | tf_op jit(solution)/shard_map/q_in/all_to_all | solution.py:200
  76.6 140.1 %all-gather.3.cloned.1.call-start = ((), (), s32[]{:S(2)}) async-start(), calls=%async_computation.13 | async-start | bytes 4718592 | tf_op jit(solution)/shard_map/kv_in/all_gather | solution.py:152
  102.9 31.5 %all-to-all-start.3 = ((bf16[8,128,1024]{1,2,0:T(8,128)(2,1)}), bf16[8,128,1024]{1,2,0:T(8,128)(2,1)}, u32[]{:S(2)}, u32[]{:S(2)}) async-start(bf16[8,128,1024]{1,2,0:T(8,128)(2,1)} %bitcast.68), calls=%async_computation.3 | async-start | bytes 4194304 | tf_op jit(solution)/shard_map/u_in/all_to_all | solution.py:200
  134.4 40.3 %all-to-all-start.2 = ((bf16[4,384,1024]{2,1,0:T(8,128)(2,1)}), bf16[4,384,1024]{2,1,0:T(8,128)(2,1)S(1)}, u32[]{:S(2)}, u32[]{:S(2)}) async-start(bf16[4,384,1024]{2,1,0:T(8,128)(2,1)} %bitcast.73), calls=%async_computation.2 | async-start | bytes 6291456 | tf_op jit(solution)/shard_map/q_in/all_to_all | solution.py:202
  174.7 1.7 copy-start
  174.7 6.6 %copy-start.6 = (s32[128]{0:T(128)S(1)}, s32[128]{0:T(128)}, u32[]{:S(2)}) copy-start(s32[128]{0:T(128)} %param.18) | copy-start | bytes 1540
  176.5 40.3 %all-to-all-start.4 = ((bf16[4,384,1024]{2,1,0:T(8,128)(2,1)}), bf16[4,384,1024]{2,1,0:T(8,128)(2,1)}, u32[]{:S(2)}, u32[]{:S(2)}) async-start(bf16[4,384,1024]{2,1,0:T(8,128)(2,1)} %bitcast.71), calls=%async_computation.4 | async-start | bytes 6291456 | tf_op jit(solution)/shard_map/u_in/all_to_all | solution.py:202
  181.1 155.9 %reduce-scatter.2.cloned.1.call-start = ((), (), s32[]{:S(2)}) async-start(), calls=%async_computation.12 | async-start | bytes 4718592 | tf_op jit(solution)/shard_map/kv_out/reduce_scatter | solution.py:212
  282.0 58.2 %all-to-all-start.7 = ((bf16[4,384,1024]{2,1,0:T(8,128)(2,1)}), bf16[4,384,1024]{2,1,0:T(8,128)(2,1)S(1)}, u32[]{:S(2)}, u32[]{:S(2)}) async-start(bf16[4,384,1024]{2,1,0:T(8,128)(2,1)} %bitcast.23), calls=%async_computation.7 | async-start | bytes 6291456 | tf_op jit(solution)/shard_map/q_out/all_to_all | solution.py:220
  340.3 28.1 %all-to-all-start.9 = ((bf16[32,48,256]{2,1,0:T(8,128)(2,1)}), bf16[32,48,256]{2,1,0:T(8,128)(2,1)}, u32[]{:S(2)}, u32[]{:S(2)}) async-start(bf16[32,48,256]{2,1,0:T(8,128)(2,1)} %bitcast.82), calls=%async_computation.10 | async-start | bytes 1572864 | tf_op jit(solution)/shard_map/kv_out/all_to_all | solution.py:214
  368.3 33.3 %all-to-all-start.8 = ((bf16[8,128,1024]{2,1,0:T(8,128)(2,1)}), bf16[8,128,1024]{2,1,0:T(8,128)(2,1)S(1)}, u32[]{:S(2)}, u32[]{:S(2)}) async-start(bf16[8,128,1024]{2,1,0:T(8,128)(2,1)} %bitcast.75), calls=%async_computation.8 | async-start | bytes 4194304 | tf_op jit(solution)/shard_map/q_out/all_to_all | solution.py:222
  401.6 13.7 %all-to-all-start.10 = ((bf16[8,128,256]{2,1,0:T(8,128)(2,1)}), bf16[8,128,256]{2,1,0:T(8,128)(2,1)S(1)}, u32[]{:S(2)}, u32[]{:S(2)}) async-start(bf16[8,128,256]{2,1,0:T(8,128)(2,1)} %bitcast.30), calls=%async_computation.11 | async-start | bytes 1048576 | tf_op jit(solution)/shard_map/kv_out/all_to_all | solution.py:216
Sparse Core Ops, SparseCore 0:
  79.2 51.1 all-gather.2
  282.1 54.8 reduce-scatter.1
